TPU v7x, 256 devices: a whole 4x4x8 slice. The times are simulated.
256 devices in a mesh: row: 32 (over y, x, core), col: 8 (over z).
Axes of the slice: x: 4, y: 4, z: 8, core: 2. Of those that a mesh axis runs over, the one named last changes fastest.
Arguments:
- inputs: bfloat16 [4096, 5120], P('row', 'col'), may hold values from -6 to 6
- grad_out: bfloat16 [4096, 5120], P('row', 'col'), may hold values from -6 to 6
- pre_act: bfloat16 [4096, 13824], P('col', 'row'), may hold values from -6 to 6
- w_in: bfloat16 [13824, 5120], P('row', 'col'), may hold values from -0.078125 to 0.078125
- w_out: bfloat16 [13824, 5120], P('row', 'col'), may hold values from -0.0546875 to 0.0546875
- row_in_prev: float32 [13824], P('row'), may hold values from 204.8 to 24576, as said below
- col_in_prev: float32 [5120], P('col'), may hold values from 204.8 to 24576, as said below
- row_out_prev: float32 [13824], P('row'), may hold values from 204.8 to 24576, as said below
- col_out_prev: float32 [5120], P('col'), may hold values from 204.8 to 24576, as said below
Outputs:
- input_grad: bfloat16 [4096, 5120], P('row', 'col')
- update_in: float32 [13824, 5120], P('row', 'col')
- row_in: float32 [13824], P('row')
- col_in: float32 [5120], P('col')
- update_out: float32 [13824, 5120], P('row', 'col')
- row_out: float32 [13824], P('row')
- col_out: float32 [5120], P('col')
Inputs may be any that keep to these rules, and one draw needn't show every extreme that they name: `row_in_prev`: positive. `col_in_prev`: positive. `row_out_prev`: positive. `col_out_prev`: positive.
All inputs are finite; a program needn't handle non-finite values.
Results may differ from a plain program's by a relative error of at most 0.023.
Values may be sent and summed in bfloat16 or wider, within the bound.
A program may use at most 128 MiB of HBM per device.

v0:
```python
import math

import jax
import jax.numpy as jnp
from jax import lax
from jax.sharding import PartitionSpec as P

D = 5120
FF = 13824


decay_rate = 0.8
epsilon_sq = 1e-30
clip_limit = 0.25
gelu_coef = 0.044715
root_coef = math.sqrt(2.0 / math.pi)


def gelu_parts(pre_float):
    tanh_value = jnp.tanh(root_coef * (pre_float + gelu_coef * pre_float * pre_float * pre_float))
    value = 0.5 * pre_float * (1.0 + tanh_value)
    slope = 0.5 * (1.0 + tanh_value) + 0.5 * pre_float * (
        1.0 - tanh_value * tanh_value
    ) * root_coef * (1.0 + 3.0 * gelu_coef * pre_float * pre_float)
    return (value, slope)


def contract_last(left, right):
    return lax.dot_general(
        left, right, (((1,), (1,)), ((), ())), preferred_element_type=jnp.float32
    )


def contract_first(left, right):
    return lax.dot_general(
        left, right, (((0,), (0,)), ((), ())), preferred_element_type=jnp.float32
    )


def row_moment(row_sum, row_prev):
    return decay_rate * row_prev + (1.0 - decay_rate) * (row_sum / D + epsilon_sq)


def col_moment(col_sum, col_prev):
    return decay_rate * col_prev + (1.0 - decay_rate) * (col_sum / FF + epsilon_sq)


def per_device(
    inputs, grad_out, pre_act, w_in, w_out, row_in_prev, col_in_prev, row_out_prev, col_out_prev
):
    grad_all, input_all = (
        lax.all_gather(grad_out, "row", axis=0, tiled=True),
        lax.all_gather(inputs, "row", axis=0, tiled=True),
    )
    token_count = float(inputs.shape[0] * lax.axis_size("row"))
    rows_here = grad_all
    hidden_grad = lax.psum_scatter(
        contract_last(rows_here, w_out).astype(jnp.bfloat16), "col", scatter_dimension=0, tiled=True
    ).astype(jnp.float32)
    value, slope = gelu_parts(pre_act.astype(jnp.float32))
    act = value.astype(jnp.bfloat16)
    pre_grad = (hidden_grad * slope).astype(jnp.bfloat16)
    act_all, pre_grad_all = (
        lax.all_gather(act, "col", axis=0, tiled=True),
        lax.all_gather(pre_grad, "col", axis=0, tiled=True),
    )
    grad_w_out = contract_first(act_all, grad_all)
    grad_w_in = contract_first(pre_grad_all, input_all)
    rows_here = pre_grad_all
    input_sum = lax.psum_scatter(
        jnp.dot(rows_here, w_in, preferred_element_type=jnp.float32).astype(jnp.bfloat16),
        "row",
        scatter_dimension=0,
        tiled=True,
    )
    square_in = grad_w_in * grad_w_in
    square_out = grad_w_out * grad_w_out
    row_sums = lax.psum((jnp.sum(square_in, axis=1), jnp.sum(square_out, axis=1)), "col")
    row_in = row_moment(row_sums[0], row_in_prev)
    row_out = row_moment(row_sums[1], row_out_prev)
    col_sums = lax.psum((jnp.sum(square_in, axis=0), jnp.sum(square_out, axis=0)), "row")
    col_in = col_moment(col_sums[0], col_in_prev)
    col_out = col_moment(col_sums[1], col_out_prev)
    raw_in = grad_w_in / jnp.sqrt(row_in[:, None] * col_in[None, :] / token_count)
    raw_out = grad_w_out / jnp.sqrt(row_out[:, None] * col_out[None, :] / token_count)
    norms = lax.psum((jnp.sum(raw_in * raw_in), jnp.sum(raw_out * raw_out)), ("row", "col"))
    total_in = norms[0]
    total_out = norms[1]
    rms_in = jnp.sqrt(total_in / (FF * D))
    rms_out = jnp.sqrt(total_out / (FF * D))
    update_in = raw_in / jnp.maximum(1.0, rms_in / clip_limit)
    update_out = raw_out / jnp.maximum(1.0, rms_out / clip_limit)
    return (input_sum, update_in, row_in, col_in, update_out, row_out, col_out)


def solution(mesh):
    return jax.shard_map(
        per_device,
        mesh=mesh,
        in_specs=(
            P("row", "col"),
            P("row", "col"),
            P("col", "row"),
            P("row", "col"),
            P("row", "col"),
            P("row"),
            P("col"),
            P("row"),
            P("col"),
        ),
        out_specs=(
            P("row", "col"),
            P("row", "col"),
            P("row"),
            P("col"),
            P("row", "col"),
            P("row"),
            P("col"),
        ),
        check_vma=False,
    )
```

profile of v0, /device:TPU:32, one launch (start us, length us, event | category | flops | bytes accessed | tf_op | source)
XLA Modules:
  0.0 451.3 jit_solution(9500882296809639069)
XLA Ops:
  7.2 0.0 copy-start
  7.2 0.0 all-gather.5.cloned.1.call-start
  7.2 0.7 all-gather.5.cloned.1.call-update
  7.9 0.0 reduce-scatter.3.cloned.1.call-start
  8.0 57.7 %all-gather.5.cloned.1.call-done = bf16[4096,640]{1,0:T(8,128)(2,1)} async-done(((bf16[128,640]{1,0:T(8,128)(2,1)}), bf16[4096,640]{1,0:T(8,128)(2,1)}) %all-gather.5.cloned.1.call-update) | async-done | bytes 5242896 | tf_op jit(solution)/shard_map/all_gather | solution.py:52
  65.7 7.4 %convolution_convert_fusion.1 = bf16[4096,432]{0,1:T(8,128)(2,1)} fusion(bf16[4096,640]{1,0:T(8,128)(2,1)} %all-gather.5.cloned.1.call-done, bf16[432,640]{1,0:T(8,128)(2,1)} %param.13), kind=kOutput, calls=%fused_computation.1 | convolution fusion | flops 2266693632 | bytes 9334784 | tf_op jit(solution)/shard_map/dot_general | solution.py:29
  73.1 0.0 copy-start.1
  73.1 0.0 reduce-scatter.3.cloned.1.call-update
  73.1 0.0 all-gather.7.cloned.1.call-start
  73.1 47.4 %reduce-scatter.3.cloned.1.call-done = bf16[512,432]{0,1:T(8,128)(2,1)} async-done(((bf16[4096,432]{0,1:T(8,128)(2,1)}), bf16[512,432]{0,1:T(8,128)(2,1)}) %reduce-scatter.3.cloned.1.call-update) | async-done | bytes 442384 | tf_op jit(solution)/shard_map/reduce_scatter | solution.py:57
  120.5 0.0 copy-done.1
  120.5 2.6 fusion.7
  123.1 0.0 all-gather.7.cloned.1.call-update
  123.1 0.0 all-gather.11.cloned.1.call-start
  123.2 0.5 all-gather.11.cloned.1.call-update
  123.7 0.0 all-gather.9.cloned.1.call-start
  123.7 0.5 all-gather.9.cloned.1.call-update
  124.3 0.0 reduce-scatter.5.cloned.1.call-start
  124.3 46.9 %all-gather.7.cloned.1.call-done = bf16[4096,432]{0,1:T(8,128)(2,1)} async-done(((bf16[512,432]{0,1:T(8,128)(2,1)}), bf16[4096,432]{0,1:T(8,128)(2,1)}) %all-gather.7.cloned.1.call-update) | async-done | bytes 3538960 | tf_op jit(solution)/shard_map/all_gather | solution.py:65
  171.2 0.0 copy-done
  171.3 7.9 %convolution_convert_fusion = bf16[4096,640]{1,0:T(8,128)(2,1)} fusion(bf16[4096,432]{0,1:T(8,128)(2,1)} %all-gather.7.cloned.1.call-done, bf16[432,640]{1,0:T(8,128)(2,1)S(1)} %copy-done), kind=kOutput, calls=%fused_computation | convolution fusion | flops 2267545600 | bytes 9334784 | tf_op jit(solution)/shard_map/dot_general | solution.py:71
  179.1 0.0 reduce-scatter.5.cloned.1.call-update
  179.1 41.8 %all-gather.11.cloned.1.call-done = bf16[4096,432]{0,1:T(8,128)(2,1)} async-done(((bf16[512,432]{0,1:T(8,128)(2,1)}), bf16[4096,432]{0,1:T(8,128)(2,1)}) %all-gather.11.cloned.1.call-update) | async-done | bytes 3538960 | tf_op jit(solution)/shard_map/all_gather | solution.py:64
  220.9 6.6 %multiply_reduce_fusion.3 = (f32[432]{0:T(512)S(1)}, f32[640]{0:T(1024)S(1)}, f32[432,640]{1,0:T(8,128)S(1)}) fusion(bf16[4096,432]{0,1:T(8,128)(2,1)} %all-gather.11.cloned.1.call-done, bf16[4096,640]{1,0:T(8,128)(2,1)} %all-gather.5.cloned.1.call-done), kind=kOutput, calls=%fused_computation.16 | convolution fusion | flops 2265752576 | bytes 9892032 | tf_op jit(solution)/shard_map/dot_general | solution.py:35
  227.5 0.0 copy-start.8
  227.5 0.0 copy-start.9
  227.5 0.0 copy-start.6
  227.5 0.0 copy-start.7
  227.5 48.4 %all-gather.9.cloned.1.call-done = bf16[4096,640]{1,0:T(8,128)(2,1)} async-done(((bf16[128,640]{1,0:T(8,128)(2,1)}), bf16[4096,640]{1,0:T(8,128)(2,1)}) %all-gather.9.cloned.1.call-update) | async-done | bytes 5242896 | tf_op jit(solution)/shard_map/all_gather | solution.py:53
  275.9 6.6 %multiply_reduce_fusion.5 = (f32[432]{0:T(512)S(1)}, f32[640]{0:T(1024)S(1)}, f32[432,640]{1,0:T(8,128)S(1)}) fusion(bf16[4096,432]{0,1:T(8,128)(2,1)} %all-gather.7.cloned.1.call-done, bf16[4096,640]{1,0:T(8,128)(2,1)} %all-gather.9.cloned.1.call-done), kind=kOutput, calls=%fused_computation.18 | convolution fusion | flops 2265752576 | bytes 9892032 | tf_op jit(solution)/shard_map/dot_general | solution.py:35
  282.5 66.7 %all-reduce.1 = (f32[640]{0:T(1024)S(1)}, f32[640]{0:T(1024)S(1)}) all-reduce(f32[640]{0:T(1024)S(1)} %get-tuple-element.10, f32[640]{0:T(1024)S(1)} %get-tuple-element.8), channel_id=1, replica_groups=mesh['row'=32,'col'=8] {'row'}, use_global_device_ids=true, to_apply=%region_5.0 | all-reduce | flops 1280 | bytes 10240 | tf_op jit(solution)/shard_map/psum | solution.py:81
  349.2 16.1 %all-reduce.2 = (f32[432]{0:T(512)S(1)}, f32[432]{0:T(512)S(1)}) all-reduce(f32[432]{0:T(512)S(1)} %get-tuple-element.9, f32[432]{0:T(512)S(1)} %get-tuple-element.7), channel_id=1, replica_groups=mesh['row'=32,'col'=8] {'col'}, use_global_device_ids=true, to_apply=%region_3.0 | all-reduce | flops 864 | bytes 6912 | tf_op jit(solution)/shard_map/psum | solution.py:78
  365.3 0.0 copy-done.8
  365.3 0.0 copy-done.9
  365.3 0.0 copy-start.4
  365.3 0.0 copy-start.5
  365.3 0.0 copy-done.6
  365.3 0.0 copy-done.7
  365.4 0.0 copy-start.2
  365.4 0.0 copy-start.3
  365.4 1.1 multiply_reduce_fusion
  366.5 1.1 multiply_reduce_fusion.1
  367.6 73.0 %all-reduce = (f32[]{:T(128)}, f32[]{:T(128)}) all-reduce(f32[]{:T(128)} %multiply_reduce_fusion.1, f32[]{:T(128)} %multiply_reduce_fusion), channel_id=1, replica_groups=mesh['row'=32,'col'=8] {'row','col'}, use_global_device_ids=true, to_apply=%region_7.0 | all-reduce | flops 2 | bytes 16 | tf_op jit(solution)/shard_map/psum | solution.py:86
  442.0 0.0 copy-done.4
  442.0 0.0 copy-done.2
  442.0 1.2 fusion.12
  443.2 0.0 copy-done.5
  443.2 0.0 copy-done.3
  443.3 1.2 fusion.11
  444.5 0.0 reduce-scatter.5.cloned.1.call-done
  (2 shorter events, 0.0 us)
Async XLA Ops:
  7.2 164.1 %copy-start = (bf16[432,640]{1,0:T(8,128)(2,1)S(1)}, bf16[432,640]{1,0:T(8,128)(2,1)}, u32[]{:S(2)}) copy-start(bf16[432,640]{1,0:T(8,128)(2,1)} %param.12) | copy-start | bytes 1658884
  7.2 58.5 %all-gather.5.cloned.1.call-start = ((), (), s32[]{:S(2)}) async-start(), calls=%async_computation.2 | async-start | bytes 5406720 | tf_op jit(solution)/shard_map/all_gather | solution.py:52
  7.9 112.6 %reduce-scatter.3.cloned.1.call-start = ((), (), s32[]{:S(2)}) async-start(), calls=%async_computation.3 | async-start | bytes 3981312 | tf_op jit(solution)/shard_map/reduce_scatter | solution.py:57
  73.1 47.5 %copy-start.1 = (bf16[512,432]{0,1:T(8,128)(2,1)S(1)}, bf16[512,432]{0,1:T(8,128)(2,1)}, u32[]{:S(2)}) copy-start(bf16[512,432]{0,1:T(8,128)(2,1)} %param.11) | copy-start | bytes 1327108
  73.1 98.2 %all-gather.7.cloned.1.call-start = ((), (), s32[]{:S(2)}) async-start(), calls=%async_computation.4 | async-start | bytes 3981312 | tf_op jit(solution)/shard_map/all_gather | solution.py:65
  123.1 97.8 %all-gather.11.cloned.1.call-start = ((), (), s32[]{:S(2)}) async-start(), calls=%async_computation.7 | async-start | bytes 3981312 | tf_op jit(solution)/shard_map/all_gather | solution.py:64
  123.7 152.2 %all-gather.9.cloned.1.call-start = ((), (), s32[]{:S(2)}) async-start(), calls=%async_computation.6 | async-start | bytes 5406720 | tf_op jit(solution)/shard_map/all_gather | solution.py:53
  124.3 320.2 %reduce-scatter.5.cloned.1.call-start = ((), (), s32[]{:S(2)}) async-start(), calls=%async_computation.5 | async-start | bytes 5406720 | tf_op jit(solution)/shard_map/reduce_scatter | solution.py:70
  227.5 137.8 %copy-start.8 = (f32[432]{0:T(512)S(1)}, f32[432]{0:T(512)}, u32[]{:S(2)}) copy-start(f32[432]{0:T(512)} %param.16) | copy-start | bytes 5188
  227.5 137.8 %copy-start.9 = (f32[432]{0:T(512)S(1)}, f32[432]{0:T(512)}, u32[]{:S(2)}) copy-start(f32[432]{0:T(512)} %param.14) | copy-start | bytes 5188
  227.5 137.8 %copy-start.6 = (f32[640]{0:T(1024)S(1)}, f32[640]{0:T(1024)}, u32[]{:S(2)}) copy-start(f32[640]{0:T(1024)} %param.17) | copy-start | bytes 7684
  227.5 137.8 %copy-start.7 = (f32[640]{0:T(1024)S(1)}, f32[640]{0:T(1024)}, u32[]{:S(2)}) copy-start(f32[640]{0:T(1024)} %param.15) | copy-start | bytes 7684
  365.3 76.7 %copy-start.4 = (f32[432]{0:T(512)}, f32[432]{0:T(512)S(1)}, u32[]{:S(2)}) copy-start(f32[432]{0:T(512)S(1)} %get-tuple-element.23) | copy-start | bytes 5188
  365.3 77.9 %copy-start.5 = (f32[432]{0:T(512)}, f32[432]{0:T(512)S(1)}, u32[]{:S(2)}) copy-start(f32[432]{0:T(512)S(1)} %get-tuple-element.24) | copy-start | bytes 5188
  365.4 76.6 %copy-start.2 = (f32[640]{0:T(1024)}, f32[640]{0:T(1024)S(1)}, u32[]{:S(2)}) copy-start(f32[640]{0:T(1024)S(1)} %get-tuple-element.21) | copy-start | bytes 7684
  365.4 77.9 %copy-start.3 = (f32[640]{0:T(1024)}, f32[640]{0:T(1024)S(1)}, u32[]{:S(2)}) copy-start(f32[640]{0:T(1024)S(1)} %get-tuple-element.22) | copy-start | bytes 7684
Sparse Core Ops, SparseCore 0:
  10.6 55.0 all-gather.4
  73.2 47.2 reduce-scatter.2
  123.2 47.9 all-gather.6
  173.6 47.2 all-gather.10
  223.6 52.2 all-gather.8
  280.9 91.6 reduce-scatter.4
where the time goes:
time: 452 us; the launch traced here: 451 us
  waiting for transfers between devices  244 us (54%)
  blocking collectives  156 us (35%)
  matrix products  28.4 us (6%)
  between operations  15.6 us (3%)
  other arithmetic  7.26 us (2%)
    psum x1, blocking collectives, per_device(): lax.psum((jnp.sum(raw_in * raw_in), jnp.sum(raw_out * raw_out)), ('row',...  73 us
    psum x1, blocking collectives, per_device(): lax.psum((jnp.sum(square_in, axis=0), jnp.sum(square_out, axis=0)), 'row')  66.7 us
    all_gather x1, waiting for transfers between devices, per_device(): lax.all_gather(grad_out, 'row', axis=0, tiled=True)  57.7 us
    all_gather x1, waiting for transfers between devices, per_device(): lax.all_gather(inputs, 'row', axis=0, tiled=True)  48.4 us
    reduce_scatter x1, waiting for transfers between devices, per_device(): lax.psum_scatter(contract_last(rows_here, w_out).astype(jnp.bfloat16), 'c...  47.4 us
    all_gather x1, waiting for transfers between devices, per_device(): lax.all_gather(pre_grad, 'col', axis=0, tiled=True)  46.9 us
    all_gather x1, waiting for transfers between devices, per_device(): lax.all_gather(act, 'col', axis=0, tiled=True)  41.8 us
    psum x1, blocking collectives, per_device(): lax.psum((jnp.sum(square_in, axis=1), jnp.sum(square_out, axis=1)), 'col')  16.1 us
  transfers between devices with their start and end apart: 6, of which 5 were waited for; matrix products, arithmetic and copies ran while one was open for 6% of the time, Pallas kernels for 0%

commit v1 on v0

v1 whole, which is shorter than its diff:
```python
import math

import jax
import jax.numpy as jnp
from jax import lax
from jax.experimental import pallas as pl
from jax.experimental.pallas import tpu as pltpu
from jax.sharding import PartitionSpec as P

D = 5120
FF = 13824
TOKENS = 4096
NY, NX, NK, NZ = 4, 4, 2, 8
TB = 128
FB = 432
DB = 640
HALF = DB // 2
QUART = DB // 4
EIGHTH = DB // 8

decay_rate = 0.8
epsilon_sq = 1e-30
clip_limit = 0.25
gelu_coef = 0.044715
root_coef = math.sqrt(2.0 / math.pi)

MESH = pl.DeviceIdType.MESH
bf16 = jnp.bfloat16
f32 = jnp.float32


def gelu_parts(p):
    t = jnp.tanh(root_coef * (p + gelu_coef * p * p * p))
    value = 0.5 * p * (1.0 + t)
    slope = 0.5 * (1.0 + t) + 0.5 * p * (1.0 - t * t) * root_coef * (
        1.0 + 3.0 * gelu_coef * p * p
    )
    return value, slope


def dot_nt(a, b):
    return lax.dot_general(a, b, (((1,), (1,)), ((), ())), preferred_element_type=f32)


def dot_nn(a, b):
    return lax.dot_general(a, b, (((1,), (0,)), ((), ())), preferred_element_type=f32)


def ring_length(h, d):
    return 4 if (h == 0) == (d == 0) else 3


SIGN = (1, -1)


def kernel(
    x_ref, g_ref, pre_ref, win_ref, wout_ref, rip_ref, cip_ref, rop_ref, cop_ref,
    ig_ref, ui_ref, ri_ref, ci_ref, uo_ref, ro_ref, co_ref,
    g_all, x_all, act_all, p_all, slope_s, hp, rs_buf, wt_s, tr_s,
    acc_out, acc_in, ipart, sib_buf, y_u, y_v, y_p, y_m, x_u, x_v, x_p, x_m,
    a2u, a2v, a2p, a2m, b2u, b2v, b2p, b2m, fin_buf, out_s,
    row_st, row_rx, prev_s, col_st, col_rx, col2_st, col2_rx,
    sc_st, sc2_st, sc3_st, sc_rx1, sc_rx2, sc_rx3,
    ssem, rsem, sib_ss, sib_rs,
):
    r = lax.axis_index("row")
    z = lax.axis_index("col")
    y = r // 8
    x = (r // 2) % 4
    k = r % 2

    def dev(yy, xx, kk, zz):
        return ((yy * 4 + xx) * 2 + kk, zz)

    def yo(o):
        return (y + (o + 4)) % 4

    def xo(o):
        return (x + (o + 4)) % 4

    def zo(o):
        return (z + (o + 8)) % 8

    sib = dev(y, x, 1 - k, z)
    xdev = {1: dev(y, xo(1), k, z), -1: dev(y, xo(-1), k, z)}
    ydev = {1: dev(yo(1), x, k, z), -1: dev(yo(-1), x, k, z)}
    zdev = {1: dev(y, x, k, zo(1)), -1: dev(y, x, k, zo(-1))}
    xk_peers = [dev(y, xo(o // 2), (k + o) % 2, z) for o in range(1, 8)]
    y_peers = [dev(yo(o), x, k, z) for o in range(1, 4)]
    z_peers = [dev(y, x, k, zo(o)) for o in range(1, 8)]

    barrier = pltpu.get_barrier_semaphore()
    everyone = xk_peers + y_peers + z_peers
    for p in everyone:
        pl.semaphore_signal(barrier, inc=1, device_id=p, device_id_type=MESH)

    count = [0]
    sent = []

    def start(src, dst, peer):
        i = count[0]
        count[0] += 1
        cp = pltpu.make_async_remote_copy(
            src_ref=src, dst_ref=dst, send_sem=ssem.at[i], recv_sem=rsem.at[i],
            device_id=peer, device_id_type=MESH,
        )
        cp.start()
        sent.append(cp)
        return i

    def arrived(i, region):
        pltpu.make_async_remote_copy(
            src_ref=region, dst_ref=region, send_sem=ssem.at[i], recv_sem=rsem.at[i],
            device_id=sib, device_id_type=MESH,
        ).wait_recv()

    def gather_stages(buf):
        lo, hi = pl.ds(0, 64), pl.ds(64, 64)

        def own(ref):
            buf[k, y, x] = ref[...]

        def p1():
            a, b = buf.at[k, y, x, lo], buf.at[k, y, x, hi]
            return [start(a, a, xdev[1]), start(a, a, xdev[-1]), start(b, b, ydev[1]), start(b, b, ydev[-1])]

        def p1f(ids):
            arrived(ids[0], buf.at[k, y, xo(-1), lo])
            s = buf.at[k, y, xo(-1), pl.ds(0, 32)]
            out = [start(s, s, xdev[1])]
            arrived(ids[1], buf.at[k, y, xo(1), lo])
            s = buf.at[k, y, xo(1), pl.ds(32, 32)]
            out.append(start(s, s, xdev[-1]))
            arrived(ids[2], buf.at[k, yo(-1), x, hi])
            s = buf.at[k, yo(-1), x, pl.ds(64, 32)]
            out.append(start(s, s, ydev[1]))
            arrived(ids[3], buf.at[k, yo(1), x, hi])
            s = buf.at[k, yo(1), x, pl.ds(96, 32)]
            out.append(start(s, s, ydev[-1]))
            return out

        def p2(ids):
            arrived(ids[0], buf.at[k, y, xo(2), pl.ds(0, 32)])
            arrived(ids[1], buf.at[k, y, xo(2), pl.ds(32, 32)])
            a = buf.at[k, y, :, lo]
            out = [start(a, a, ydev[1]), start(a, a, ydev[-1])]
            arrived(ids[2], buf.at[k, yo(2), x, pl.ds(64, 32)])
            arrived(ids[3], buf.at[k, yo(2), x, pl.ds(96, 32)])
            b = buf.at[k, :, x, hi]
            return out + [start(b, b, xdev[1]), start(b, b, xdev[-1])]

        def p2f(ids):
            arrived(ids[0], buf.at[k, yo(-1), :, lo])
            s = buf.at[k, yo(-1), pl.ds(0, 2), lo]
            out = [start(s, s, ydev[1])]
            arrived(ids[1], buf.at[k, yo(1), :, lo])
            s = buf.at[k, yo(1), pl.ds(2, 2), lo]
            out.append(start(s, s, ydev[-1]))
            arrived(ids[2], buf.at[k, :, xo(-1), hi])
            s = buf.at[k, pl.ds(0, 2), xo(-1), hi]
            out.append(start(s, s, xdev[1]))
            arrived(ids[3], buf.at[k, :, xo(1), hi])
            s = buf.at[k, pl.ds(2, 2), xo(1), hi]
            out.append(start(s, s, xdev[-1]))
            return out

        def to_sib(ids):
            arrived(ids[0], buf.at[k, yo(2), pl.ds(0, 2), lo])
            arrived(ids[1], buf.at[k, yo(2), pl.ds(2, 2), lo])
            arrived(ids[2], buf.at[k, pl.ds(0, 2), xo(2), hi])
            arrived(ids[3], buf.at[k, pl.ds(2, 2), xo(2), hi])
            return [start(buf.at[k], buf.at[k], sib)]

        def done(ids):
            arrived(ids[0], buf.at[1 - k])

        return own, p1, p1f, p2, p2f, to_sib, done

    def ring_send(buf, h, d, s):
        piece = buf.at[h, zo(-SIGN[d] * (s - 1))]
        return start(piece, piece, zdev[SIGN[d]])

    def ring_wait(buf, ids, h, d, s):
        arrived(ids[h, d, s], buf.at[h, zo(-SIGN[d] * s)])

    def ring_step(buf, ids, s):
        for h in range(2):
            for d in range(2):
                if s <= ring_length(h, d):
                    ring_wait(buf, ids, h, d, s)
                    if s + 1 <= ring_length(h, d):
                        ids[h, d, s + 1] = ring_send(buf, h, d, s + 1)

    pl.semaphore_wait(barrier, len(everyone))

    g_own, g_p1, g_p1f, g_p2, g_p2f, g_sib, g_done = gather_stages(g_all)
    x_own, x_p1, x_p1f, x_p2, x_p2f, x_sib, x_done = gather_stages(x_all)

    g_own(g_ref)
    gi = g_p1()
    act_ids = {}
    for h in range(2):
        for q in range(2):
            j = q * 2 + h
            value, slope = gelu_parts(pre_ref[:, j * TB:(j + 1) * TB].astype(f32))
            act_all[h, z, :, q * TB:(q + 1) * TB] = value.astype(bf16)
            slope_s[h, :, q * TB:(q + 1) * TB] = slope
        for d in range(2):
            act_ids[h, d, 1] = ring_send(act_all, h, d, 1)
    gi = g_p1f(gi)
    x_own(x_ref)
    tr_s[...] = jnp.zeros_like(tr_s)
    tr_s[0:FB, :] = win_ref[...].astype(f32)
    for q in range(5):
        wt_s[q * TB:(q + 1) * TB, :] = jnp.transpose(tr_s[:, q * TB:(q + 1) * TB])[:, 0:FB].astype(bf16)
    gi = g_p2(gi)
    ring_step(act_all, act_ids, 1)
    gi = g_p2f(gi)
    gi = g_sib(gi)
    xi = x_p1()
    ring_step(act_all, act_ids, 2)
    xi = x_p1f(xi)
    xi = x_p2(xi)
    ring_step(act_all, act_ids, 3)
    g_done(gi)

    def tokens(buf, h, zz):
        return buf[h, zz // 2, pl.ds((zz % 2) * 2, 2)].reshape(2 * TB, DB)

    def partial_products(lo_i, hi_i):
        def body(i, _):
            h = i % 2
            q = i // 2
            o = 4 - (q % 2) * ((q + 1) // 2) + (1 - q % 2) * (q // 2)
            zz = (z + o) % 8
            hp[h, zz] = dot_nt(wout_ref[...], tokens(g_all, h, zz)).astype(bf16)
            return 0

        lax.fori_loop(lo_i, hi_i, body, 0)

    rs_ids = {}

    def rs_send(h, d, s):
        n = ring_length(h, d)
        dest = zo(SIGN[d] * (n - s + 1))
        if s == 1:
            src = hp.at[h, dest]
        else:
            src = rs_buf.at[h, d, s - 2]
            arrived(rs_ids[h, d, s - 1], src)
            rs_buf[h, d, s - 2] = (
                rs_buf[h, d, s - 2].astype(f32) + hp[h, dest].astype(f32)
            ).astype(bf16)
        rs_ids[h, d, s] = start(src, rs_buf.at[h, d, s - 1], zdev[SIGN[d]])

    def rs_step(s):
        for h in range(2):
            for d in range(2):
                if s <= ring_length(h, d):
                    rs_send(h, d, s)

    partial_products(0, 6)
    rs_step(1)
    partial_products(6, 16)
    xi = x_p2f(xi)
    rs_step(2)

    ring_step(act_all, act_ids, 4)

    def wgrad(acc, left, right, lo_i, hi_i):
        def body(i, _):
            acc[...] += dot_nn(left[0, i], tokens(right, 0, i)) + dot_nn(left[1, i], tokens(right, 1, i))
            return 0

        lax.fori_loop(lo_i, hi_i, body, 0)

    acc_out[...] = jnp.zeros_like(acc_out)
    wgrad(acc_out, act_all, g_all, 0, 4)
    rs_step(3)
    xi = x_sib(xi)
    wgrad(acc_out, act_all, g_all, 4, 8)
    rs_step(4)

    def square_sums(acc, off_row, off_col):
        total = jnp.zeros((FB, 1), f32)
        for q in range(5):
            c = slice(q * TB, (q + 1) * TB)
            v = acc[:, c]
            v = v * v
            col_st[0:1, off_col + q * TB:off_col + (q + 1) * TB] = jnp.sum(v, axis=0, keepdims=True)
            total += jnp.sum(v, axis=1, keepdims=True)
        tr_s[0:FB, 0:TB] = jnp.broadcast_to(total, (FB, TB))
        row_st[0:1, off_row:off_row + 512] = jnp.transpose(tr_s[:, 0:TB])[0:1, :]

    square_sums(acc_out, 512, 640)

    p_ids = {}
    for h in range(2):
        total = hp[h, z].astype(f32)
        for d in range(2):
            n = ring_length(h, d)
            arrived(rs_ids[h, d, n], rs_buf.at[h, d, n - 1])
            total += rs_buf[h, d, n - 1].astype(f32)
        p_all[h, z] = (total * slope_s[h]).astype(bf16)
        for d in range(2):
            p_ids[h, d, 1] = ring_send(p_all, h, d, 1)
    x_done(xi)

    acc_in[...] = jnp.zeros_like(acc_in)

    def sib_copy(h, zz):
        yy, x0 = zz // 2, (zz % 2) * 2
        return pltpu.make_async_remote_copy(
            src_ref=ipart.at[h, yy, pl.ds(x0, 2), pl.ds((1 - k) * HALF, HALF)],
            dst_ref=sib_buf.at[h, yy, pl.ds(x0, 2)],
            send_sem=sib_ss.at[h, zz], recv_sem=sib_rs.at[h, zz],
            device_id=sib, device_id_type=MESH,
        )

    def consume(h, zz):
        yy, x0 = zz // 2, (zz % 2) * 2
        pt = p_all[h, zz]
        part = dot_nn(wt_s[...], pt)
        ipart[h, yy, x0] = part[:, 0:TB].astype(bf16)
        ipart[h, yy, x0 + 1] = part[:, TB:2 * TB].astype(bf16)
        sib_copy(h, zz).start()
        acc_in[...] += dot_nn(pt, tokens(x_all, h, zz))

    def join(h, zz):
        yy, x0 = zz // 2, (zz % 2) * 2
        sib_copy(h, zz).wait_recv()
        rows = pl.ds(pl.multiple_of(k * HALF, HALF), HALF)
        for q in range(2):
            ipart[h, yy, x0 + q, rows, :] = (
                ipart[h, yy, x0 + q, rows, :].astype(f32) + sib_buf[h, yy, x0 + q].astype(f32)
            ).astype(bf16)

    def blocks(fn, s):
        if s == 0:
            def body(i, _):
                fn(i, z)
                return 0
            lax.fori_loop(0, 2, body, 0)
        elif s < 4:
            def body(i, _):
                h = i // 2
                fn(h, (z + 8 + (2 * (i % 2) - 1) * s) % 8)
                return 0
            lax.fori_loop(0, 4, body, 0)
        else:
            def body(i, _):
                fn(i, (z + 4) % 8)
                return 0
            lax.fori_loop(0, 2, body, 0)

    blocks(consume, 0)
    for s in range(1, 5):
        ring_step(p_all, p_ids, s)
        blocks(consume, s)
        blocks(join, s - 1)
    blocks(join, 4)

    base = pl.multiple_of(k * HALF, HALF)

    def feature_rows(off, size):
        return pl.ds(pl.multiple_of(base + off, 16), size)

    a_rows, b_rows = feature_rows(0, QUART), feature_rows(QUART, QUART)
    au, av = feature_rows(0, EIGHTH), feature_rows(EIGHTH, EIGHTH)
    bu, bv = feature_rows(QUART, EIGHTH), feature_rows(QUART + EIGHTH, EIGHTH)

    def add_to(view, *others):
        v = view[...].astype(f32)
        for o in others:
            v += o[...].astype(f32)
        view[...] = v.astype(bf16)

    def ring4(slab, off, devs, ru, rv, rp, rm, rows_all, rows_u, rows_v):
        def s1():
            return [
                start(slab(off(2), rows_u), ru, devs[1]),
                start(slab(off(2), rows_v), rv, devs[-1]),
            ]

        def s2(ids):
            arrived(ids[0], ru)
            add_to(slab(off(1), rows_u), ru)
            out = [start(slab(off(1), rows_all), rp, devs[1])]
            arrived(ids[1], rv)
            add_to(slab(off(-1), rows_v), rv)
            return out + [start(slab(off(-1), rows_all), rm, devs[-1])]

        def s3(ids):
            arrived(ids[0], rp)
            arrived(ids[1], rm)
            add_to(slab(off(0), rows_all), rp, rm)

        return s1, s2, s3

    ya = ring4(lambda o, rr: ipart.at[:, o, :, rr], yo, ydev, y_u, y_v, y_p, y_m, a_rows, au, av)
    xb = ring4(lambda o, rr: ipart.at[:, :, o, rr], xo, xdev, x_u, x_v, x_p, x_m, b_rows, bu, bv)
    xa = ring4(lambda o, rr: ipart.at[:, y, o, rr], xo, xdev, a2u, a2v, a2p, a2m, a_rows, au, av)
    yb = ring4(lambda o, rr: ipart.at[:, o, x, rr], yo, ydev, b2u, b2v, b2p, b2m, b_rows, bu, bv)

    i1, i2 = ya[0](), xb[0]()
    square_sums(acc_in, 0, 0)

    xk_slots = [xo(-(o // 2)) * 2 + (k + o) % 2 for o in range(1, 8)]
    y_slots = [yo(-o) for o in range(1, 4)]
    z_slots = [zo(-o) for o in range(1, 8)]

    def exchange(src, rx, me, peers):
        rx[me] = src[...]
        return [start(src, rx.at[me], p) for p in peers]

    def collect(ids, rx, slots, n):
        for i, slot in zip(ids, slots):
            arrived(i, rx.at[slot])
        total = rx[0]
        for j in range(1, n):
            total += rx[j]
        return total

    row_ids = exchange(row_st, row_rx, z, z_peers)
    col_ids = exchange(col_st, col_rx, x * 2 + k, xk_peers)
    i1, i2 = ya[1](i1), xb[1](i2)
    col2_st[...] = collect(col_ids, col_rx, xk_slots, 8)
    col_ids = exchange(col2_st, col2_rx, y, y_peers)
    row_sum = collect(row_ids, row_rx, z_slots, 8)
    prev_s[...] = jnp.ones_like(prev_s)
    prev_s[0:1, 0:FB] = rip_ref[...]
    prev_s[0:1, 512:512 + FB] = rop_ref[...]
    row_new = decay_rate * prev_s[...] + (1.0 - decay_rate) * (row_sum / D + epsilon_sq)
    ri_ref[...] = row_new[:, 0:FB]
    ro_ref[...] = row_new[:, 512:512 + FB]
    row_f = 1.0 / jnp.sqrt(row_new)
    ya[2](i1)
    xb[2](i2)
    i1, i2 = xa[0](), yb[0]()
    col_sum = collect(col_ids, col2_rx, y_slots, 4)
    col_in = decay_rate * cip_ref[...] + (1.0 - decay_rate) * (col_sum[:, 0:DB] / FF + epsilon_sq)
    col_out = decay_rate * cop_ref[...] + (1.0 - decay_rate) * (col_sum[:, DB:2 * DB] / FF + epsilon_sq)
    ci_ref[...] = col_in
    co_ref[...] = col_out
    root_tokens = math.sqrt(TOKENS)

    def raw_update(acc, out_ref, row_part, col, off):
        rows = jnp.transpose(jnp.broadcast_to(row_part, (TB, 512)))[0:FB, :]
        factor = root_tokens / jnp.sqrt(col)
        total = jnp.zeros((1, TB), f32)
        for q in range(5):
            c = slice(q * TB, (q + 1) * TB)
            v = acc[:, c] * (rows * factor[:, c])
            out_ref[:, c] = v
            total += jnp.sum(v * v, axis=0, keepdims=True)
        sc_st[0:1, off:off + TB] = total

    raw_update(acc_in, ui_ref, row_f[:, 0:512], col_in, 0)
    raw_update(acc_out, uo_ref, row_f[:, 512:1024], col_out, TB)
    sc_ids = exchange(sc_st, sc_rx1, x * 2 + k, xk_peers)
    i1, i2 = xa[1](i1), yb[1](i2)
    sc2_st[...] = collect(sc_ids, sc_rx1, xk_slots, 8)
    sc_ids = exchange(sc2_st, sc_rx2, y, y_peers)
    xa[2](i1)
    yb[2](i2)
    half = pl.ds(pl.multiple_of(k * HALF, HALF), HALF)
    fin = start(ipart.at[1 - k, y, x, half], fin_buf, sib)
    sc3_st[...] = collect(sc_ids, sc_rx2, y_slots, 4)
    sc_ids = exchange(sc3_st, sc_rx3, z, z_peers)
    out_s[half, :] = ipart[k, y, x, half, :].astype(f32)
    arrived(fin, fin_buf)
    other = pl.ds(pl.multiple_of((1 - k) * HALF, HALF), HALF)
    out_s[other, :] = fin_buf[...].astype(f32)
    for q in range(5):
        c = slice(q * TB, (q + 1) * TB)
        ig_ref[:, c] = jnp.transpose(out_s[c, :]).astype(bf16)
    sc = collect(sc_ids, sc_rx3, z_slots, 8)

    def clip(out_ref, part):
        total = jnp.sum(part, axis=1, keepdims=True)
        rms = jnp.sqrt(total / (FF * D))
        out_ref[...] = out_ref[...] * (1.0 / jnp.maximum(1.0, rms / clip_limit))

    clip(ui_ref, sc[:, 0:TB])
    clip(uo_ref, sc[:, TB:2 * TB])

    for cp in sent:
        cp.wait_send()

    def drain(i, _):
        sib_copy(i // 8, i % 8).wait_send()
        return 0

    lax.fori_loop(0, 16, drain, 0)


COPIES = 128


def per_device(
    inputs, grad_out, pre_act, w_in, w_out, row_in_prev, col_in_prev, row_out_prev, col_out_prev
):
    vmem = pl.BlockSpec(memory_space=pltpu.VMEM)

    def v(*shape, dtype=bf16):
        return pltpu.VMEM(shape, dtype)

    outs = pl.pallas_call(
        kernel,
        out_shape=(
            jax.ShapeDtypeStruct((TB, DB), bf16),
            jax.ShapeDtypeStruct((FB, DB), f32),
            jax.ShapeDtypeStruct((1, FB), f32),
            jax.ShapeDtypeStruct((1, DB), f32),
            jax.ShapeDtypeStruct((FB, DB), f32),
            jax.ShapeDtypeStruct((1, FB), f32),
            jax.ShapeDtypeStruct((1, DB), f32),
        ),
        in_specs=[vmem] * 9,
        out_specs=[vmem] * 7,
        scratch_shapes=[
            v(2, 4, 4, TB, DB), v(2, 4, 4, TB, DB),
            v(2, 8, FB, 256), v(2, 8, FB, 256),
            v(2, FB, 256, dtype=f32),
            v(2, 8, FB, 256),
            v(2, 2, 4, FB, 256),
            v(DB, FB), v(512, DB, dtype=f32),
            v(FB, DB, dtype=f32), v(FB, DB, dtype=f32),
            v(2, 4, 4, DB, TB), v(2, 4, 4, HALF, TB),
            v(2, 4, EIGHTH, TB), v(2, 4, EIGHTH, TB), v(2, 4, QUART, TB), v(2, 4, QUART, TB),
            v(2, 4, EIGHTH, TB), v(2, 4, EIGHTH, TB), v(2, 4, QUART, TB), v(2, 4, QUART, TB),
            v(2, EIGHTH, TB), v(2, EIGHTH, TB), v(2, QUART, TB), v(2, QUART, TB),
            v(2, EIGHTH, TB), v(2, EIGHTH, TB), v(2, QUART, TB), v(2, QUART, TB),
            v(HALF, TB), v(DB, TB, dtype=f32),
            v(1, 1024, dtype=f32), v(8, 1, 1024, dtype=f32), v(1, 1024, dtype=f32),
            v(1, 1280, dtype=f32), v(8, 1, 1280, dtype=f32),
            v(1, 1280, dtype=f32), v(4, 1, 1280, dtype=f32),
            v(1, 256, dtype=f32), v(1, 256, dtype=f32), v(1, 256, dtype=f32),
            v(8, 1, 256, dtype=f32), v(4, 1, 256, dtype=f32), v(8, 1, 256, dtype=f32),
            pltpu.SemaphoreType.DMA((COPIES,)), pltpu.SemaphoreType.DMA((COPIES,)),
            pltpu.SemaphoreType.DMA((2, 8)), pltpu.SemaphoreType.DMA((2, 8)),
        ],
        compiler_params=pltpu.CompilerParams(
            collective_id=0, has_side_effects=True, vmem_limit_bytes=60 * 1024 * 1024
        ),
        name="ffn_backward",
    )(
        inputs, grad_out, pre_act.T, w_in, w_out,
        row_in_prev[None], col_in_prev[None], row_out_prev[None], col_out_prev[None],
    )
    ig, ui, ri, ci, uo, ro, co = outs
    return ig, ui, ri[0], ci[0], uo, ro[0], co[0]


def solution(mesh):
    return jax.shard_map(
        per_device,
        mesh=mesh,
        in_specs=(
            P("row", "col"),
            P("row", "col"),
            P("col", "row"),
            P("row", "col"),
            P("row", "col"),
            P("row"),
            P("col"),
            P("row"),
            P("col"),
        ),
        out_specs=(
            P("row", "col"),
            P("row", "col"),
            P("row"),
            P("col"),
            P("row", "col"),
            P("row"),
            P("col"),
        ),
        check_vma=False,
    )
```

time: 452 us -> 164 us (0.36)
  waiting for transfers between devices: 244 us -> 0 us
  blocking collectives: 156 us -> 0 us
  Pallas kernels: 0 us -> 151 us
  matrix products: 28.4 us -> 0 us
  between operations: 15.6 us -> 0.65 us
  local copies, waits for them, and re-layouts: 0.06 us -> 8.68 us
  other arithmetic: 7.26 us -> 2.55 us
    all_gather x4 -> x0, waiting for transfers between devices: 195 us -> none  [the longest x1 57.7 us: per_device(): lax.all_gather(grad_out, 'row', axis=0, tiled=True)]
    psum x3 -> x0, blocking collectives: 156 us -> none  [the longest x1 73 us: per_device(): lax.psum((jnp.sum(raw_in * raw_in), jnp.sum(raw_out * raw_out)), ('row',...]
    pallas_call x0 -> x1, Pallas kernels: none -> 151 us  [per_device(): pl.pallas_call(kernel, out_shape=(jax.ShapeDtypeStruct((TB, DB), bf16), j...]
    reduce_scatter x2 -> x0, waiting for transfers between devices: 47.4 us -> none  [the longest x1 47.4 us: per_device(): lax.psum_scatter(contract_last(rows_here, w_out).astype(jnp.bfloat16), 'c...]
    dot_general x4 -> x0, matrix products: 28.4 us -> none  [the longest x2 13.1 us: contract_first(): lax.dot_general(left, right, (((0,), (0,)), ((), ())), preferred_element_...]
    unnamed x20 -> x11, local copies, waits for them, and re-layouts: 0.06 us -> 6.15 us
  transfers between devices with their start and end apart: 6 -> 0, of which waited for: 5 -> 0; matrix products, arithmetic and copies ran while one was open for 6% -> 0% of each run, Pallas kernels for 0% -> 0%
where the time goes in v1:
time: 164 us; the launch traced here: 163 us
  Pallas kernels  151 us (92%)
  local copies, waits for them, and re-layouts  8.68 us (5%)
  other arithmetic  2.55 us (2%)
    pallas_call x1, Pallas kernels, per_device(): pl.pallas_call(kernel, out_shape=(jax.ShapeDtypeStruct((TB, DB), bf16), j...  151 us
    unnamed x11, local copies, waits for them, and re-layouts  6.15 us

profile of v1, /device:TPU:32, one launch (start us, length us, event | category | flops | bytes accessed | tf_op | source)
XLA Modules:
  0.0 163.3 jit_solution(2774067707186367825)
XLA Ops:
  0.6 1.3 broadcast_in_dim.13.cip_ref
  1.9 1.3 broadcast_in_dim.15.cop_ref
  3.2 151.4 %ffn_backward.1 = (bf16[128,640]{1,0:T(8,128)(2,1)}, f32[432,640]{1,0:T(8,128)}, f32[1,432]{1,0:T(1,128)}, f32[1,640]{1,0:T(1,128)}, f32[432,640]{1,0:T(8,128)}, /*index=5*/f32[1,432]{1,0:T(1,128)}, f32[1,640]{1,0:T(1,128)}) custom-call(bf16[128,640]{1,0:T(8,128)(2,1)} %x_ref.1, bf16[128,640]{1,0:T(8,128)(2,1)} %g_ref.1, bf16[432,512]{1,0:T(8,128)(2,1)} %bitcast.5, ...), custom_call_target="tpu_custom_call" | custom-call | tf_op jit(solution)/shard_map/ffn_backward/pallas_call | solution.py:508
  154.6 1.3 reduce
  155.9 1.3 reduce.1
  157.1 1.6 copy.21
  158.7 0.0 copy-start.2
  158.7 0.0 copy-start
  158.7 2.4 %copy.22 = f32[432,640]{1,0:T(8,128)} copy(f32[432,640]{1,0:T(8,128)} %get-tuple-element.29) | data formatting | bytes 2211840
  161.1 0.0 copy-done.2
  161.1 0.6 copy.23
  161.7 0.0 copy-done
  161.7 0.0 copy-start.1
  161.7 1.0 copy.24
  162.7 0.0 copy-done.1
  162.7 0.6 copy.25
Async XLA Ops:
  158.7 2.4 %copy-start.2 = (f32[1,432]{1,0:T(1,128)S(1)}, f32[1,432]{1,0:T(1,128)}, u32[]{:S(2)}) copy-start(f32[1,432]{1,0:T(1,128)} %get-tuple-element.16) | copy-start | bytes 5188
  158.7 3.0 %copy-start = (f32[432,640]{1,0:T(8,128)S(1)}, f32[432,640]{1,0:T(8,128)}, u32[]{:S(2)}) copy-start(f32[432,640]{1,0:T(8,128)} %get-tuple-element.32) | copy-start | bytes 3317764
  161.7 1.0 copy-start.1

commit v2 on v1

v2 whole, which is shorter than its diff:
```python
import math

import jax
import jax.numpy as jnp
from jax import lax
from jax.experimental import pallas as pl
from jax.experimental.pallas import tpu as pltpu
from jax.sharding import PartitionSpec as P

D = 5120
FF = 13824
TOKENS = 4096
NY, NX, NK, NZ = 4, 4, 2, 8
TB = 128
FB = 432
DB = 640
HALF = DB // 2
QUART = DB // 4
EIGHTH = DB // 8

decay_rate = 0.8
epsilon_sq = 1e-30
clip_limit = 0.25
gelu_coef = 0.044715
root_coef = math.sqrt(2.0 / math.pi)

MESH = pl.DeviceIdType.MESH
bf16 = jnp.bfloat16
f32 = jnp.float32


def gelu_parts(p):
    t = jnp.tanh(root_coef * (p + gelu_coef * p * p * p))
    value = 0.5 * p * (1.0 + t)
    slope = 0.5 * (1.0 + t) + 0.5 * p * (1.0 - t * t) * root_coef * (
        1.0 + 3.0 * gelu_coef * p * p
    )
    return value, slope


def dot_nt(a, b):
    return lax.dot_general(a, b, (((1,), (1,)), ((), ())), preferred_element_type=f32)


def dot_nn(a, b):
    return lax.dot_general(a, b, (((1,), (0,)), ((), ())), preferred_element_type=f32)


def dot_tn(a, b):
    return lax.dot_general(a, b, (((0,), (0,)), ((), ())), preferred_element_type=f32)


def kernel(
    x_ref, g_ref, pre_ref, win_ref, wout_ref, rip_ref, cip_ref, rop_ref, cop_ref,
    ig_ref, ui_ref, uo_ref, rows_ref, cols_ref, sums_ref,
    g_all, x_all, act_all, p_all, slope_s, hp, rs_buf, pre_s, win_s, wout_s, tr_s,
    acc_out, acc_in, ipart, sib_buf, y_u, y_v, y_p, y_m, x_u, x_v, x_p, x_m,
    a2u, a2v, a2p, a2m, b2u, b2v, b2p, b2m, fin_buf, out_s, ig_s,
    rip_s, cip_s, rop_s, cop_s, rows_o, cols_o, sums_o,
    row_st, row_rx, col_st, col_rx, col2_st, col2_rx,
    sc_st, sc2_st, sc3_st, sc_rx1, sc_rx2, sc_rx3,
    ssem, rsem, sib_ss, sib_rs, act_ss, act_rs, p_ss, p_rs, h_ss, h_rs, io_sem,
):
    r = lax.axis_index("row")
    z = lax.axis_index("col")
    y = r // 8
    x = (r // 2) % 4
    k = r % 2

    def dev(yy, xx, kk, zz):
        return ((yy * 4 + xx) * 2 + kk, zz)

    def yo(o):
        return (y + (o + 4)) % 4

    def xo(o):
        return (x + (o + 4)) % 4

    def zo(o):
        return (z + (o + 8)) % 8

    sib = dev(y, x, 1 - k, z)
    xdev = {1: dev(y, xo(1), k, z), -1: dev(y, xo(-1), k, z)}
    ydev = {1: dev(yo(1), x, k, z), -1: dev(yo(-1), x, k, z)}
    xk_peers = [dev(y, xo(o // 2), (k + o) % 2, z) for o in range(1, 8)]
    y_peers = [dev(yo(o), x, k, z) for o in range(1, 4)]
    z_peers = [dev(y, x, k, zo(o)) for o in range(1, 8)]

    barrier = pltpu.get_barrier_semaphore()
    everyone = xk_peers + y_peers + z_peers
    for p in everyone:
        pl.semaphore_signal(barrier, inc=1, device_id=p, device_id_type=MESH)

    loads = {}
    for i, (name, src, dst) in enumerate((
        ("g", g_ref, g_all.at[k, y, x]),
        ("pre", pre_ref, pre_s),
        ("wout", wout_ref, wout_s),
        ("x", x_ref, x_all.at[k, y, x]),
        ("win", win_ref, win_s),
        ("rip", rip_ref, rip_s),
        ("rop", rop_ref, rop_s),
        ("cip", cip_ref, cip_s),
        ("cop", cop_ref, cop_s),
    )):
        loads[name] = pltpu.make_async_copy(src, dst, io_sem.at[i])
        loads[name].start()

    count = [0]
    sent = []

    def start(src, dst, peer):
        i = count[0]
        count[0] += 1
        cp = pltpu.make_async_remote_copy(
            src_ref=src, dst_ref=dst, send_sem=ssem.at[i], recv_sem=rsem.at[i],
            device_id=peer, device_id_type=MESH,
        )
        cp.start()
        sent.append(cp)
        return i

    def arrived(i, region):
        pltpu.make_async_remote_copy(
            src_ref=region, dst_ref=region, send_sem=ssem.at[i], recv_sem=rsem.at[i],
            device_id=sib, device_id_type=MESH,
        ).wait_recv()

    def gather_stages(buf):
        lo, hi = pl.ds(0, 64), pl.ds(64, 64)
        shared = []

        def share(view):
            shared.append((start(view(k), view(k), sib), view))

        def p1():
            a, b = buf.at[k, y, x, lo], buf.at[k, y, x, hi]
            return [start(a, a, xdev[1]), start(a, a, xdev[-1]), start(b, b, ydev[1]), start(b, b, ydev[-1])]

        def p1f(ids):
            arrived(ids[0], buf.at[k, y, xo(-1), lo])
            s = buf.at[k, y, xo(-1), pl.ds(0, 32)]
            out = [start(s, s, xdev[1])]
            arrived(ids[1], buf.at[k, y, xo(1), lo])
            s = buf.at[k, y, xo(1), pl.ds(32, 32)]
            out.append(start(s, s, xdev[-1]))
            arrived(ids[2], buf.at[k, yo(-1), x, hi])
            s = buf.at[k, yo(-1), x, pl.ds(64, 32)]
            out.append(start(s, s, ydev[1]))
            arrived(ids[3], buf.at[k, yo(1), x, hi])
            s = buf.at[k, yo(1), x, pl.ds(96, 32)]
            out.append(start(s, s, ydev[-1]))
            return out

        def p2(ids):
            arrived(ids[0], buf.at[k, y, xo(2), pl.ds(0, 32)])
            arrived(ids[1], buf.at[k, y, xo(2), pl.ds(32, 32)])
            a = buf.at[k, y, :, lo]
            out = [start(a, a, ydev[1]), start(a, a, ydev[-1])]
            arrived(ids[2], buf.at[k, yo(2), x, pl.ds(64, 32)])
            arrived(ids[3], buf.at[k, yo(2), x, pl.ds(96, 32)])
            b = buf.at[k, :, x, hi]
            out += [start(b, b, xdev[1]), start(b, b, xdev[-1])]
            share(lambda kk: buf.at[kk, y, :, lo])
            share(lambda kk: buf.at[kk, :, x, hi])
            return out

        def p2f(ids):
            arrived(ids[0], buf.at[k, yo(-1), :, lo])
            s = buf.at[k, yo(-1), pl.ds(0, 2), lo]
            out = [start(s, s, ydev[1])]
            arrived(ids[1], buf.at[k, yo(1), :, lo])
            s = buf.at[k, yo(1), pl.ds(2, 2), lo]
            out.append(start(s, s, ydev[-1]))
            arrived(ids[2], buf.at[k, :, xo(-1), hi])
            s = buf.at[k, pl.ds(0, 2), xo(-1), hi]
            out.append(start(s, s, xdev[1]))
            arrived(ids[3], buf.at[k, :, xo(1), hi])
            s = buf.at[k, pl.ds(2, 2), xo(1), hi]
            out.append(start(s, s, xdev[-1]))
            share(lambda kk: buf.at[kk, yo(-1), :, lo])
            share(lambda kk: buf.at[kk, yo(1), :, lo])
            share(lambda kk: buf.at[kk, :, xo(-1), hi])
            share(lambda kk: buf.at[kk, :, xo(1), hi])
            return out

        def last(ids):
            arrived(ids[0], buf.at[k, yo(2), pl.ds(0, 2), lo])
            arrived(ids[1], buf.at[k, yo(2), pl.ds(2, 2), lo])
            share(lambda kk: buf.at[kk, yo(2), :, lo])
            arrived(ids[2], buf.at[k, pl.ds(0, 2), xo(2), hi])
            arrived(ids[3], buf.at[k, pl.ds(2, 2), xo(2), hi])
            share(lambda kk: buf.at[kk, :, xo(2), hi])

        def done():
            for i, view in shared:
                arrived(i, view(1 - k))

        return p1, p1f, p2, p2f, last, done

    def stream(u):
        s = u // 4
        j = u % 4
        h = j % 2
        d = (j % 2 + j // 2) % 2
        return s, j, h, 1 - 2 * d

    def block(u):
        s, _, h, sign = stream(u)
        return h, (z + 8 - sign * s) % 8

    def ring_peer(sign):
        return (r, (z + 8 + sign) % 8)

    def ag_copy(buf, ss, rs, u):
        s, _, h, sign = stream(u)
        piece = buf.at[h, (z + 8 - sign * (s - 1)) % 8]
        return pltpu.make_async_remote_copy(
            src_ref=piece, dst_ref=piece, send_sem=ss.at[u], recv_sem=rs.at[u],
            device_id=ring_peer(sign), device_id_type=MESH,
        )

    def ag_wait(buf, ss, rs, u):
        h, zz = block(u)
        piece = buf.at[h, zz]
        pltpu.make_async_remote_copy(
            src_ref=piece, dst_ref=piece, send_sem=ss.at[u], recv_sem=rs.at[u],
            device_id=sib, device_id_type=MESH,
        ).wait_recv()

    act = (act_all, act_ss, act_rs)
    pg = (p_all, p_ss, p_rs)

    def act_pass(lo_u, hi_u):
        def body(u, _):
            ag_wait(*act, u)
            ag_copy(*act, u + 4).start()
            return 0

        lax.fori_loop(lo_u, hi_u, body, 0)

    g_p1, g_p1f, g_p2, g_p2f, g_last, g_done = gather_stages(g_all)
    x_p1, x_p1f, x_p2, x_p2f, x_last, x_done = gather_stages(x_all)

    loads["g"].wait()
    pl.semaphore_wait(barrier, len(everyone))
    gi = g_p1()
    loads["pre"].wait()
    for h in range(2):
        for q in range(2):
            j = q * 2 + h
            value, slope = gelu_parts(pre_s[:, j * TB:(j + 1) * TB].astype(f32))
            act_all[h, z, :, q * TB:(q + 1) * TB] = value.astype(bf16)
            slope_s[h, :, q * TB:(q + 1) * TB] = slope
        ag_copy(*act, 4 + h).start()
        ag_copy(*act, 6 + h).start()
    gi = g_p1f(gi)
    gi = g_p2(gi)
    act_pass(4, 8)
    gi = g_p2f(gi)
    loads["x"].wait()
    xi = x_p1()
    tr_s[...] = jnp.zeros_like(tr_s)
    act_pass(8, 10)
    g_last(gi)
    loads["wout"].wait()
    g_done()

    def tokens(buf, h, zz):
        return buf[h, zz // 2, pl.ds((zz % 2) * 2, 2)].reshape(2 * TB, DB)

    def partial_products(lo_i, hi_i):
        def body(i, _):
            h = i % 2
            q = i // 2
            o = 4 - (q % 2) * ((q + 1) // 2) + (1 - q % 2) * (q // 2)
            zz = (z + o) % 8
            hp[h, zz] = dot_nt(wout_s[...], tokens(g_all, h, zz)).astype(bf16)
            return 0

        lax.fori_loop(lo_i, hi_i, body, 0)

    def rs_dest(u):
        s, j, h, sign = stream(u)
        return h, (z + 8 + sign * (5 - j // 2 - s)) % 8, sign

    def rs_copy(src, u):
        _, _, sign = rs_dest(u)
        return pltpu.make_async_remote_copy(
            src_ref=src, dst_ref=rs_buf.at[u - 4], send_sem=h_ss.at[u], recv_sem=h_rs.at[u],
            device_id=ring_peer(sign), device_id_type=MESH,
        )

    def rs_first(u, _):
        h, dest, _ = rs_dest(u)
        rs_copy(hp.at[h, dest], u).start()
        return 0

    def rs_wait(u):
        rs_copy(rs_buf.at[u - 4], u).wait_recv()

    def wgrad_block(acc, left, right, u):
        h, zz = block(u)
        acc[...] += dot_nn(left[h, zz], tokens(right, h, zz))

    def rs_next(u, _):
        h, dest, _ = rs_dest(u)
        rs_wait(u - 4)
        rs_buf[u - 8] = (rs_buf[u - 8].astype(f32) + hp[h, dest].astype(f32)).astype(bf16)
        rs_copy(rs_buf.at[u - 8], u).start()

        @pl.when(u < 16)
        def _():
            wgrad_block(acc_out, act_all, g_all, u - 6)

        return 0

    partial_products(0, 6)
    lax.fori_loop(4, 8, rs_first, 0)
    xi = x_p1f(xi)
    xi = x_p2(xi)
    partial_products(6, 16)
    acc_out[...] = jnp.zeros_like(acc_out)
    acc_in[...] = jnp.zeros_like(acc_in)
    lax.fori_loop(8, 12, rs_next, 0)
    xi = x_p2f(xi)
    lax.fori_loop(12, 18, rs_next, 0)
    x_last(xi)

    for h in range(2):
        total = hp[h, z].astype(f32)
        for u in (14 + h, 16 + h):
            rs_wait(u)
            total += rs_buf[u - 4].astype(f32)
        p_all[h, z] = (total * slope_s[h]).astype(bf16)
        ag_copy(*pg, 4 + h).start()
        ag_copy(*pg, 6 + h).start()
    loads["win"].wait()
    x_done()

    base = pl.multiple_of(k * HALF, HALF)
    half = pl.ds(base, HALF)
    other = pl.ds(pl.multiple_of((1 - k) * HALF, HALF), HALF)

    def sib_copy(h, zz):
        yy, x0 = zz // 2, (zz % 2) * 2
        return pltpu.make_async_remote_copy(
            src_ref=ipart.at[h, yy, pl.ds(x0, 2), other],
            dst_ref=sib_buf.at[h, yy, pl.ds(x0, 2)],
            send_sem=sib_ss.at[h, zz], recv_sem=sib_rs.at[h, zz],
            device_id=sib, device_id_type=MESH,
        )

    def consume(u):
        h, zz = block(u)
        yy, x0 = zz // 2, (zz % 2) * 2
        pt = p_all[h, zz]
        part = dot_tn(win_s[...], pt)
        ipart[h, yy, x0] = part[:, 0:TB].astype(bf16)
        ipart[h, yy, x0 + 1] = part[:, TB:2 * TB].astype(bf16)
        sib_copy(h, zz).start()
        acc_in[...] += dot_nn(pt, tokens(x_all, h, zz))

    def join(u):
        h, zz = block(u)
        yy, x0 = zz // 2, (zz % 2) * 2
        sib_copy(h, zz).wait_recv()
        for q in range(2):
            ipart[h, yy, x0 + q, half, :] = (
                ipart[h, yy, x0 + q, half, :].astype(f32) + sib_buf[h, yy, x0 + q].astype(f32)
            ).astype(bf16)

    def p_step(u, _):
        @pl.when(u >= 4)
        def _():
            ag_wait(*pg, u)

        @pl.when((u >= 4) & (u < 14))
        def _():
            ag_copy(*pg, u + 4).start()

        @pl.when(u >= 14)
        def _():
            ag_wait(*act, u - 4)
            ag_copy(*act, u).start()

        consume(u)

        @pl.when(u >= 5)
        def _():
            join(u - 3)

        return 0

    lax.fori_loop(2, 18, p_step, 0)

    def join_step(u, _):
        join(u)
        return 0

    lax.fori_loop(15, 18, join_step, 0)

    def feature_rows(off, size):
        return pl.ds(pl.multiple_of(base + off, 16), size)

    a_rows, b_rows = feature_rows(0, QUART), feature_rows(QUART, QUART)
    au, av = feature_rows(0, EIGHTH), feature_rows(EIGHTH, EIGHTH)
    bu, bv = feature_rows(QUART, EIGHTH), feature_rows(QUART + EIGHTH, EIGHTH)

    def add_to(view, *others):
        v = view[...].astype(f32)
        for o in others:
            v += o[...].astype(f32)
        view[...] = v.astype(bf16)

    def ring4(slab, off, devs, ru, rv, rp, rm, rows_all, rows_u, rows_v):
        def s1():
            return [
                start(slab(off(2), rows_u), ru, devs[1]),
                start(slab(off(2), rows_v), rv, devs[-1]),
            ]

        def s2(ids):
            arrived(ids[0], ru)
            add_to(slab(off(1), rows_u), ru)
            out = [start(slab(off(1), rows_all), rp, devs[1])]
            arrived(ids[1], rv)
            add_to(slab(off(-1), rows_v), rv)
            return out + [start(slab(off(-1), rows_all), rm, devs[-1])]

        def s3(ids):
            arrived(ids[0], rp)
            arrived(ids[1], rm)
            add_to(slab(off(0), rows_all), rp, rm)

        return s1, s2, s3

    ya = ring4(lambda o, rr: ipart.at[:, o, :, rr], yo, ydev, y_u, y_v, y_p, y_m, a_rows, au, av)
    xb = ring4(lambda o, rr: ipart.at[:, :, o, rr], xo, xdev, x_u, x_v, x_p, x_m, b_rows, bu, bv)
    xa = ring4(lambda o, rr: ipart.at[:, y, o, rr], xo, xdev, a2u, a2v, a2p, a2m, a_rows, au, av)
    yb = ring4(lambda o, rr: ipart.at[:, o, x, rr], yo, ydev, b2u, b2v, b2p, b2m, b_rows, bu, bv)

    i1, i2 = ya[0](), xb[0]()

    def square_sums(acc, off_row, off_col):
        total = jnp.zeros((FB, 1), f32)
        for q in range(5):
            c = slice(q * TB, (q + 1) * TB)
            v = acc[:, c]
            v = v * v
            col_st[0:1, off_col + q * TB:off_col + (q + 1) * TB] = jnp.sum(v, axis=0, keepdims=True)
            total += jnp.sum(v, axis=1, keepdims=True)
        tr_s[0:FB, :] = jnp.broadcast_to(total, (FB, TB))
        row_st[0:1, off_row:off_row + 512] = jnp.transpose(tr_s[...])[0:1, :]

    def wgrad_step(u, _):
        wgrad_block(acc_out, act_all, g_all, u)
        return 0

    lax.fori_loop(10, 14, wgrad_step, 0)
    square_sums(acc_in, 0, 0)
    i1, i2 = ya[1](i1), xb[1](i2)

    def act_last(u, _):
        ag_wait(*act, u)
        wgrad_block(acc_out, act_all, g_all, u)
        return 0

    lax.fori_loop(14, 18, act_last, 0)
    square_sums(acc_out, 512, 640)

    xk_slots = [xo(-(o // 2)) * 2 + (k + o) % 2 for o in range(1, 8)]
    y_slots = [yo(-o) for o in range(1, 4)]
    z_slots = [zo(-o) for o in range(1, 8)]

    def exchange(src, rx, me, peers):
        rx[me] = src[...]
        return [start(src, rx.at[me], p) for p in peers]

    def collect(ids, rx, slots, n):
        for i, slot in zip(ids, slots):
            arrived(i, rx.at[slot])
        total = rx[0]
        for j in range(1, n):
            total += rx[j]
        return total

    col_ids = exchange(col_st, col_rx, x * 2 + k, xk_peers)
    row_ids = exchange(row_st, row_rx, z, z_peers)
    ya[2](i1)
    xb[2](i2)
    i1, i2 = xa[0](), yb[0]()
    for name in ("rip", "rop", "cip", "cop"):
        loads[name].wait()
    col2_st[...] = collect(col_ids, col_rx, xk_slots, 8)
    col_ids = exchange(col2_st, col2_rx, y, y_peers)
    i1, i2 = xa[1](i1), yb[1](i2)
    row_sum = collect(row_ids, row_rx, z_slots, 8)

    def moment(prev, part, n):
        prev = prev[...].reshape(1, prev.shape[0])
        return decay_rate * prev + (1.0 - decay_rate) * (part / n + epsilon_sq)

    rows_o[...] = jnp.ones_like(rows_o)
    rows_o[0:1, 0:FB] = moment(rip_s, row_sum[:, 0:FB], D)
    rows_o[0:1, 512:512 + FB] = moment(rop_s, row_sum[:, 512:512 + FB], D)
    row_f = 1.0 / jnp.sqrt(rows_o[...])
    col_sum = collect(col_ids, col2_rx, y_slots, 4)
    cols_o[0:1, 0:DB] = moment(cip_s, col_sum[:, 0:DB], FF)
    cols_o[0:1, DB:2 * DB] = moment(cop_s, col_sum[:, DB:2 * DB], FF)
    root_tokens = math.sqrt(TOKENS)

    stores = []

    def store(src, dst):
        cp = pltpu.make_async_copy(src, dst, io_sem.at[9 + len(stores)])
        cp.start()
        stores.append(cp)

    store(rows_o, rows_ref)
    store(cols_o, cols_ref)

    def raw_update(acc, out_ref, row_part, col, off):
        rows = jnp.transpose(jnp.broadcast_to(row_part, (TB, 512)))[0:FB, :]
        factor = root_tokens / jnp.sqrt(col)
        total = jnp.zeros((1, TB), f32)
        for q in range(5):
            c = slice(q * TB, (q + 1) * TB)
            v = acc[:, c] * (rows * factor[:, c])
            acc[:, c] = v
            total += jnp.sum(v * v, axis=0, keepdims=True)
        sc_st[0:1, off:off + TB] = total
        store(acc, out_ref)

    raw_update(acc_in, ui_ref, row_f[:, 0:512], cols_o[0:1, 0:DB], 0)
    raw_update(acc_out, uo_ref, row_f[:, 512:1024], cols_o[0:1, DB:2 * DB], TB)
    sc_ids = exchange(sc_st, sc_rx1, x * 2 + k, xk_peers)
    xa[2](i1)
    yb[2](i2)
    fin = start(ipart.at[1 - k, y, x, half], fin_buf, sib)
    sc2_st[...] = collect(sc_ids, sc_rx1, xk_slots, 8)
    sc_ids = exchange(sc2_st, sc_rx2, y, y_peers)
    out_s[half, :] = ipart[k, y, x, half, :].astype(f32)
    arrived(fin, fin_buf)
    out_s[other, :] = fin_buf[...].astype(f32)
    for q in range(5):
        c = slice(q * TB, (q + 1) * TB)
        ig_s[:, c] = jnp.transpose(out_s[c, :]).astype(bf16)
    store(ig_s, ig_ref)
    sc3_st[...] = collect(sc_ids, sc_rx2, y_slots, 4)
    sc_ids = exchange(sc3_st, sc_rx3, z, z_peers)
    for cp in sent[:-len(z_peers)]:
        cp.wait_send()

    def drain(u, _):
        ag_copy(*act, u).wait_send()
        ag_copy(*pg, u).wait_send()
        rs_copy(rs_buf.at[u - 4], u).wait_send()
        return 0

    lax.fori_loop(4, 18, drain, 0)

    def sib_drain(i, _):
        sib_copy(i // 8, i % 8).wait_send()
        return 0

    lax.fori_loop(0, 16, sib_drain, 0)
    sums_o[...] = collect(sc_ids, sc_rx3, z_slots, 8)
    store(sums_o, sums_ref)
    for cp in sent[-len(z_peers):]:
        cp.wait_send()
    for cp in stores:
        cp.wait()


def finish(
    ig_in, ui_in, uo_in, rows, cols, sums,
    ig_ref, ui_ref, ri_ref, ci_ref, uo_ref, ro_ref, co_ref,
):
    ig_ref[...] = ig_in[...]

    def clip(raw, out_ref, part):
        total = jnp.sum(part, axis=1, keepdims=True)
        rms = jnp.sqrt(total / (FF * D))
        out_ref[...] = raw[...] * (1.0 / jnp.maximum(1.0, rms / clip_limit))

    clip(ui_in, ui_ref, sums[0:1, 0:TB])
    clip(uo_in, uo_ref, sums[0:1, TB:2 * TB])
    ri_ref[...] = rows[0:1, 0:FB].reshape(FB)
    ro_ref[...] = rows[0:1, 512:512 + FB].reshape(FB)
    ci_ref[...] = cols[0:1, 0:DB].reshape(DB)
    co_ref[...] = cols[0:1, DB:2 * DB].reshape(DB)


COPIES = 128


def per_device(
    inputs, grad_out, pre_act, w_in, w_out, row_in_prev, col_in_prev, row_out_prev, col_out_prev
):
    hbm = pl.BlockSpec(memory_space=pl.ANY)
    vmem = pl.BlockSpec(memory_space=pltpu.VMEM)
    dma = pltpu.SemaphoreType.DMA

    def v(*shape, dtype=bf16):
        return pltpu.VMEM(shape, dtype)

    ig, ui, uo, rows, cols, sums = pl.pallas_call(
        kernel,
        out_shape=(
            jax.ShapeDtypeStruct((TB, DB), bf16),
            jax.ShapeDtypeStruct((FB, DB), f32),
            jax.ShapeDtypeStruct((FB, DB), f32),
            jax.ShapeDtypeStruct((1, 1024), f32),
            jax.ShapeDtypeStruct((1, 1280), f32),
            jax.ShapeDtypeStruct((1, 256), f32),
        ),
        in_specs=[hbm] * 9,
        out_specs=[hbm] * 6,
        scratch_shapes=[
            v(2, 4, 4, TB, DB), v(2, 4, 4, TB, DB),
            v(2, 8, FB, 256), v(2, 8, FB, 256),
            v(2, FB, 256, dtype=f32),
            v(2, 8, FB, 256),
            v(14, FB, 256),
            v(FB, 512), v(FB, DB), v(FB, DB),
            v(512, TB, dtype=f32),
            v(FB, DB, dtype=f32), v(FB, DB, dtype=f32),
            v(2, 4, 4, DB, TB), v(2, 4, 4, HALF, TB),
            v(2, 4, EIGHTH, TB), v(2, 4, EIGHTH, TB), v(2, 4, QUART, TB), v(2, 4, QUART, TB),
            v(2, 4, EIGHTH, TB), v(2, 4, EIGHTH, TB), v(2, 4, QUART, TB), v(2, 4, QUART, TB),
            v(2, EIGHTH, TB), v(2, EIGHTH, TB), v(2, QUART, TB), v(2, QUART, TB),
            v(2, EIGHTH, TB), v(2, EIGHTH, TB), v(2, QUART, TB), v(2, QUART, TB),
            v(HALF, TB), v(DB, TB, dtype=f32), v(TB, DB),
            v(FB, dtype=f32), v(DB, dtype=f32), v(FB, dtype=f32), v(DB, dtype=f32),
            v(1, 1024, dtype=f32), v(1, 1280, dtype=f32), v(1, 256, dtype=f32),
            v(1, 1024, dtype=f32), v(8, 1, 1024, dtype=f32),
            v(1, 1280, dtype=f32), v(8, 1, 1280, dtype=f32),
            v(1, 1280, dtype=f32), v(4, 1, 1280, dtype=f32),
            v(1, 256, dtype=f32), v(1, 256, dtype=f32), v(1, 256, dtype=f32),
            v(8, 1, 256, dtype=f32), v(4, 1, 256, dtype=f32), v(8, 1, 256, dtype=f32),
            dma((COPIES,)), dma((COPIES,)), dma((2, 8)), dma((2, 8)),
            dma((18,)), dma((18,)), dma((18,)), dma((18,)), dma((18,)), dma((18,)), dma((16,)),
        ],
        compiler_params=pltpu.CompilerParams(
            collective_id=0, has_side_effects=True, vmem_limit_bytes=60 * 1024 * 1024
        ),
        name="ffn_backward",
    )(
        inputs, grad_out, pre_act.T, w_in, w_out,
        row_in_prev, col_in_prev, row_out_prev, col_out_prev,
    )
    return pl.pallas_call(
        finish,
        out_shape=(
            jax.ShapeDtypeStruct((TB, DB), bf16),
            jax.ShapeDtypeStruct((FB, DB), f32),
            jax.ShapeDtypeStruct((FB,), f32),
            jax.ShapeDtypeStruct((DB,), f32),
            jax.ShapeDtypeStruct((FB, DB), f32),
            jax.ShapeDtypeStruct((FB,), f32),
            jax.ShapeDtypeStruct((DB,), f32),
        ),
        in_specs=[vmem] * 6,
        out_specs=[vmem] * 7,
        compiler_params=pltpu.CompilerParams(vmem_limit_bytes=60 * 1024 * 1024),
        name="clip_updates",
    )(ig, ui, uo, rows, cols, sums)


def solution(mesh):
    return jax.shard_map(
        per_device,
        mesh=mesh,
        in_specs=(
            P("row", "col"),
            P("row", "col"),
            P("col", "row"),
            P("row", "col"),
            P("row", "col"),
            P("row"),
            P("col"),
            P("row"),
            P("col"),
        ),
        out_specs=(
            P("row", "col"),
            P("row", "col"),
            P("row"),
            P("col"),
            P("row", "col"),
            P("row"),
            P("col"),
        ),
        check_vma=False,
    )
```

time: 164 us -> 148 us (0.902)
  local copies, waits for them, and re-layouts: 8.68 us -> 0 us
  Pallas kernels: 151 us -> 148 us
  other arithmetic: 2.55 us -> 0 us
    pallas_call x1, Pallas kernels: 151 us -> 144 us  [per_device(): pl.pallas_call(kernel, out_shape=(jax.ShapeDtypeStruct((TB, DB), bf16), j...]
    unnamed x11 -> x0, local copies, waits for them, and re-layouts: 6.15 us -> none
    pallas_call x0 -> x1, Pallas kernels: none -> 3.17 us  [per_device(): pl.pallas_call(finish, out_shape=(jax.ShapeDtypeStruct((TB, DB), bf16), j...]
    pallas_call x2 -> x0, other arithmetic: 2.55 us -> none  [per_device(): pl.pallas_call(kernel, out_shape=(jax.ShapeDtypeStruct((TB, DB), bf16), j...]
    broadcast_in_dim x2 -> x0, local copies, waits for them, and re-layouts: 2.53 us -> none  [the longest x1 1.27 us: per_device(): col_in_prev[None]]
where the time goes in v2:
time: 148 us
  Pallas kernels  148 us (100%)
    pallas_call x1, Pallas kernels, per_device(): pl.pallas_call(kernel, out_shape=(jax.ShapeDtypeStruct((TB, DB), bf16), j...  144 us
    pallas_call x1, Pallas kernels, per_device(): pl.pallas_call(finish, out_shape=(jax.ShapeDtypeStruct((TB, DB), bf16), j...  3.17 us

profile of v2, /device:TPU:32, one launch (start us, length us, event | category | flops | bytes accessed | tf_op | source)
XLA Modules:
  0.0 148.2 jit_solution(17624496396009229829)
XLA Ops:
  0.6 144.4 %ffn_backward.1 = (bf16[128,640]{1,0:T(8,128)(2,1)}, f32[432,640]{1,0:T(8,128)}, f32[432,640]{1,0:T(8,128)}, f32[1,1024]{1,0:T(1,128)}, f32[1,1280]{1,0:T(1,128)}, /*index=5*/f32[1,256]{1,0:T(1,128)}) custom-call(bf16[128,640]{1,0:T(8,128)(2,1)} %x_ref.1, bf16[128,640]{1,0:T(8,128)(2,1)} %g_ref.1, bf16[432,512]{1,0:T(8,128)(2,1)} %bitcast.1, ...), custom_call_target="tpu_custom_call" | custom-call | tf_op jit(solution)/shard_map/ffn_backward/pallas_call | solution.py:608
  145.0 3.2 %clip_updates.1 = (bf16[128,640]{1,0:T(8,128)(2,1)}, f32[432,640]{1,0:T(8,128)}, f32[432]{0:T(512)}, f32[640]{0:T(1024)}, f32[432,640]{1,0:T(8,128)}, /*index=5*/f32[432]{0:T(512)}, f32[640]{0:T(1024)}) custom-call(bf16[128,640]{1,0:T(8,128)(2,1)} %get-tuple-element.13.ig_in, f32[432,640]{1,0:T(8,128)} %get-tuple-element.14.ui_in, ...), custom_call_target="tpu_custom_call" | custom-call | tf_op jit(solution)/shard_map/clip_updates/pallas_call | solution.py:653

commit v3 on v2

--- a/solution.py
+++ b/solution.py
@@ -253,8 +253,9 @@
             act_all[h, z, :, q * TB:(q + 1) * TB] = value.astype(bf16)
             slope_s[h, :, q * TB:(q + 1) * TB] = slope
         ag_copy(*act, 4 + h).start()
-        ag_copy(*act, 6 + h).start()
     gi = g_p1f(gi)
+    ag_copy(*act, 6).start()
+    ag_copy(*act, 7).start()
     gi = g_p2(gi)
     act_pass(4, 8)
     gi = g_p2f(gi)
@@ -315,8 +316,10 @@
 
         return 0
 
-    partial_products(0, 6)
-    lax.fori_loop(4, 8, rs_first, 0)
+    partial_products(0, 2)
+    lax.fori_loop(4, 6, rs_first, 0)
+    partial_products(2, 6)
+    lax.fori_loop(6, 8, rs_first, 0)
     xi = x_p1f(xi)
     xi = x_p2(xi)
     partial_products(6, 16)
@@ -334,7 +337,6 @@
             total += rs_buf[u - 4].astype(f32)
         p_all[h, z] = (total * slope_s[h]).astype(bf16)
         ag_copy(*pg, 4 + h).start()
-        ag_copy(*pg, 6 + h).start()
     loads["win"].wait()
     x_done()
 
@@ -359,7 +361,10 @@
         ipart[h, yy, x0] = part[:, 0:TB].astype(bf16)
         ipart[h, yy, x0 + 1] = part[:, TB:2 * TB].astype(bf16)
         sib_copy(h, zz).start()
-        acc_in[...] += dot_nn(pt, tokens(x_all, h, zz))
+
+        @pl.when(u < 14)
+        def _():
+            wgrad_block(acc_in, p_all, x_all, u)
 
     def join(u):
         h, zz = block(u)
@@ -385,6 +390,11 @@
             ag_copy(*act, u).start()
 
         consume(u)
+
+        @pl.when(u == 3)
+        def _():
+            ag_copy(*pg, 6).start()
+            ag_copy(*pg, 7).start()
 
         @pl.when(u >= 5)
         def _():
@@ -457,9 +467,14 @@
         wgrad_block(acc_out, act_all, g_all, u)
         return 0
 
-    lax.fori_loop(10, 14, wgrad_step, 0)
+    def wgrad_in_step(u, _):
+        wgrad_block(acc_in, p_all, x_all, u)
+        return 0
+
+    lax.fori_loop(14, 18, wgrad_in_step, 0)
     square_sums(acc_in, 0, 0)
     i1, i2 = ya[1](i1), xb[1](i2)
+    lax.fori_loop(10, 14, wgrad_step, 0)
 
     def act_last(u, _):
         ag_wait(*act, u)
@@ -487,6 +502,23 @@
 
     col_ids = exchange(col_st, col_rx, x * 2 + k, xk_peers)
     row_ids = exchange(row_st, row_rx, z, z_peers)
+
+    def drain(u, _):
+        ag_copy(*act, u).wait_send()
+        ag_copy(*pg, u).wait_send()
+        rs_copy(rs_buf.at[u - 4], u).wait_send()
+        return 0
+
+    lax.fori_loop(4, 18, drain, 0)
+
+    def sib_drain(i, _):
+        sib_copy(i // 8, i % 8).wait_send()
+        return 0
+
+    lax.fori_loop(0, 16, sib_drain, 0)
+    early = len(sent)
+    for cp in sent[:early - 18]:
+        cp.wait_send()
     ya[2](i1)
     xb[2](i2)
     i1, i2 = xa[0](), yb[0]()
@@ -549,25 +581,9 @@
     store(ig_s, ig_ref)
     sc3_st[...] = collect(sc_ids, sc_rx2, y_slots, 4)
     sc_ids = exchange(sc3_st, sc_rx3, z, z_peers)
-    for cp in sent[:-len(z_peers)]:
-        cp.wait_send()
-
-    def drain(u, _):
-        ag_copy(*act, u).wait_send()
-        ag_copy(*pg, u).wait_send()
-        rs_copy(rs_buf.at[u - 4], u).wait_send()
-        return 0
-
-    lax.fori_loop(4, 18, drain, 0)
-
-    def sib_drain(i, _):
-        sib_copy(i // 8, i % 8).wait_send()
-        return 0
-
-    lax.fori_loop(0, 16, sib_drain, 0)
     sums_o[...] = collect(sc_ids, sc_rx3, z_slots, 8)
     store(sums_o, sums_ref)
-    for cp in sent[-len(z_peers):]:
+    for cp in sent[early - 18:]:
         cp.wait_send()
     for cp in stores:
         cp.wait()
@@ -599,7 +615,11 @@
     inputs, grad_out, pre_act, w_in, w_out, row_in_prev, col_in_prev, row_out_prev, col_out_prev
 ):
     hbm = pl.BlockSpec(memory_space=pl.ANY)
-    vmem = pl.BlockSpec(memory_space=pltpu.VMEM)
+    strip = pl.BlockSpec((FB // 3, DB), lambda i: (i, 0))
+
+    def whole(*shape):
+        return pl.BlockSpec(shape, lambda i: (0,) * len(shape))
+
     dma = pltpu.SemaphoreType.DMA
 
     def v(*shape, dtype=bf16):
@@ -661,8 +681,9 @@
             jax.ShapeDtypeStruct((FB,), f32),
             jax.ShapeDtypeStruct((DB,), f32),
         ),
-        in_specs=[vmem] * 6,
-        out_specs=[vmem] * 7,
+        grid=(3,),
+        in_specs=[whole(TB, DB), strip, strip, whole(1, 1024), whole(1, 1280), whole(1, 256)],
+        out_specs=[whole(TB, DB), strip, whole(FB), whole(DB), strip, whole(FB), whole(DB)],
         compiler_params=pltpu.CompilerParams(vmem_limit_bytes=60 * 1024 * 1024),
         name="clip_updates",
     )(ig, ui, uo, rows, cols, sums)

time: 148 us -> 147 us (level)
  Pallas kernels: 148 us -> 145 us
    pallas_call x1, Pallas kernels: 144 us -> 141 us  [per_device(): pl.pallas_call(kernel, out_shape=(jax.ShapeDtypeStruct((TB, DB), bf16), j...]
where the time goes in v3:
time: 147 us; the launch traced here: 146 us
  Pallas kernels  145 us (99%)
    pallas_call x1, Pallas kernels, per_device(): pl.pallas_call(kernel, out_shape=(jax.ShapeDtypeStruct((TB, DB), bf16), j...  141 us
    pallas_call x1, Pallas kernels, per_device(): pl.pallas_call(finish, out_shape=(jax.ShapeDtypeStruct((TB, DB), bf16), j...  3.96 us

profile of v3, /device:TPU:32, one launch (start us, length us, event | category | flops | bytes accessed | tf_op | source)
XLA Modules:
  0.0 145.8 jit_solution(11126409828316106953)
XLA Ops:
  0.6 141.2 %ffn_backward.1 = (bf16[128,640]{1,0:T(8,128)(2,1)}, f32[432,640]{1,0:T(8,128)}, f32[432,640]{1,0:T(8,128)}, f32[1,1024]{1,0:T(1,128)}, f32[1,1280]{1,0:T(1,128)}, /*index=5*/f32[1,256]{1,0:T(1,128)}) custom-call(bf16[128,640]{1,0:T(8,128)(2,1)} %x_ref.1, bf16[128,640]{1,0:T(8,128)(2,1)} %g_ref.1, bf16[432,512]{1,0:T(8,128)(2,1)} %bitcast.1, ...), custom_call_target="tpu_custom_call" | custom-call | tf_op jit(solution)/shard_map/ffn_backward/pallas_call | solution.py:628
  141.8 4.0 %clip_updates.1 = (bf16[128,640]{1,0:T(8,128)(2,1)}, f32[432,640]{1,0:T(8,128)}, f32[432]{0:T(512)}, f32[640]{0:T(1024)}, f32[432,640]{1,0:T(8,128)}, /*index=5*/f32[432]{0:T(512)}, f32[640]{0:T(1024)}) custom-call(bf16[128,640]{1,0:T(8,128)(2,1)} %get-tuple-element.13.ig_in, f32[432,640]{1,0:T(8,128)} %get-tuple-element.14.ui_in, ...), custom_call_target="tpu_custom_call" | custom-call | tf_op jit(solution)/shard_map/clip_updates/pallas_call | solution.py:673
